TPU v7x, 128 devices: a whole 4x4x4 slice. The times are simulated.
128 devices in a mesh: req: 16 (over x, y), row: 8 (over z, core).
Axes of the slice: x: 4, y: 4, z: 4, core: 2. Of those that a mesh axis runs over, the one named last changes fastest.
Arguments:
- patches: bfloat16 [8, 2048, 1280], P('row', 'req'), may hold values from -6 to 6
- picture_ids: int32 [8, 2048], P('row'), may hold values from -1 to 15, as said below
- ln_attn: float32 [1280], replicated, may hold values from 0.1 to 1.9
- w_qkv: bfloat16 [3, 1280, 1280], P(None, None, 'req'), may hold values from -6 to 6
- w_out: bfloat16 [1280, 1280], P('req'), may hold values from -1.25 to 1.25
- ln_mlp: float32 [1280], replicated, may hold values from 0.1 to 1.9
- w_up: bfloat16 [1280, 5120], P(None, 'req'), may hold values from -0.15625 to 0.15625
- w_down: bfloat16 [5120, 1280], P('req'), may hold values from -0.3125 to 0.3125
- w_merge: bfloat16 [5120, 1280], replicated, may hold values from -0.078125 to 0.078125
- text_embed: bfloat16 [16384, 1280], P(('req', 'row')), may hold values from -6 to 6
- slot_dest: int32 [8, 512], P('row', 'req'), may hold values from -1 to 16383, as said below
Outputs:
- prompt_embed: bfloat16 [16384, 1280], P(('req', 'row'))
Inputs may be any that keep to these rules, and one draw needn't show every extreme that they name: `picture_ids`: each group holds whole pictures one after another from its first row, each picture's length a multiple of 4 and laid out so that every aligned run of four rows is one 2x2 window; rows after the last picture are padding. `slot_dest`: A merged row has a prompt row exactly when its patch rows belong to a picture; no prompt row is named twice; a merged row of group g (rows of the row index g) names a prompt row of a device with the same row index; at most 2 merged rows of one device name prompt rows of one device, and in every draw some device sends that many to one device.
All inputs are finite; a program needn't handle non-finite values.
Results may differ from a plain program's by a relative error of at most 0.023.
Values may be sent and summed in bfloat16 or wider, within the bound.
No kernel may reach another device: no remote copies, remote signals or barrier semaphores. Data moves between devices by JAX's collectives and lax.ppermute only.
A program may use at most 128 MiB of HBM per device.

v0:
```python
import math
import jax
import jax.numpy as jnp
from jax import lax
from jax.sharding import PartitionSpec as P

HEAD = 80


def layer_norm(rows, gain):
    rows32 = rows.astype(jnp.float32)
    center = rows32 - jnp.mean(rows32, axis=-1, keepdims=True)
    spread = jnp.mean(center * center, axis=-1, keepdims=True)
    return center * lax.rsqrt(spread + 1e-06) * gain


def local(
    patches,
    picture_ids,
    ln_attn,
    w_qkv,
    w_out,
    ln_mlp,
    w_up,
    w_down,
    w_merge,
    text_embed,
    slot_dest,
):
    rows = patches[0]
    local_rows = rows.shape[0]
    width = rows.shape[1]
    ids = picture_ids[0]
    group_rows = ids.shape[0]
    head_cols = w_out.shape[0]
    req_count = lax.axis_size("req")
    row_count = lax.axis_size("row")
    normed = layer_norm(rows, ln_attn).astype(jnp.bfloat16)
    qkv = jnp.einsum(
        "rd,tdc->trc",
        lax.all_gather(normed, "req", axis=0, tiled=True),
        w_qkv,
        preferred_element_type=jnp.float32,
    ).astype(jnp.bfloat16)
    keys = qkv[1]
    values = qkv[2]
    block = min(512, group_rows)
    blocks = group_rows // block
    scale = 1.0 / math.sqrt(HEAD)

    def attend(item):
        query_block, id_block = item
        same = id_block[:, None] == ids[None, :]
        scores = (
            jnp.einsum("qc,kc->qk", query_block, keys, preferred_element_type=jnp.float32) * scale
        )
        scores = jnp.where(same, scores, -1e30)
        top = jnp.max(scores, axis=1, keepdims=True)
        expo = jnp.exp(scores - top)
        probs = (expo / jnp.sum(expo, axis=1, keepdims=True)).astype(jnp.bfloat16)
        results = [jnp.dot(probs, values, preferred_element_type=jnp.float32).astype(jnp.bfloat16)]
        return jnp.concatenate(results, axis=1)

    attended = lax.map(
        attend, (qkv[0].reshape(blocks, block, head_cols), ids.reshape(blocks, block))
    )
    attended = attended.reshape(group_rows, head_cols)
    piece = lax.slice_in_dim(attended, 0, local_rows * lax.axis_size("req"), axis=0)
    attn = lax.psum_scatter(
        jnp.dot(piece, w_out, preferred_element_type=jnp.float32).astype(jnp.bfloat16),
        "req",
        scatter_dimension=0,
        tiled=True,
    ).astype(jnp.float32)
    resid = (rows.astype(jnp.float32) + attn).astype(jnp.bfloat16)
    normed_two = layer_norm(resid, ln_mlp).astype(jnp.bfloat16)
    hidden = jax.nn.gelu(
        jnp.dot(
            lax.all_gather(normed_two, "req", axis=0, tiled=True),
            w_up,
            preferred_element_type=jnp.float32,
        ),
        approximate=False,
    ).astype(jnp.bfloat16)
    piece = lax.slice_in_dim(hidden, 0, local_rows * lax.axis_size("req"), axis=0)
    mlp = lax.psum_scatter(
        jnp.dot(piece, w_down, preferred_element_type=jnp.float32).astype(jnp.bfloat16),
        "req",
        scatter_dimension=0,
        tiled=True,
    ).astype(jnp.float32)
    vision = (resid.astype(jnp.float32) + mlp).astype(jnp.bfloat16)
    merged = vision.reshape(local_rows // 4, 4 * width)
    merged_count = merged.shape[0]
    dest = slot_dest[0]
    prompt_rows = text_embed.shape[0]
    slot_cap = max(2, merged_count // req_count)
    owner = jnp.where(dest >= 0, dest // prompt_rows // row_count, -1)
    order = jnp.arange(merged_count)
    same_owner = (owner[:, None] == owner[None, :]) & (order[None, :] < order[:, None])
    ranks = jnp.sum(same_owner.astype(jnp.int32), axis=1)
    target = jnp.where(owner >= 0, owner * slot_cap + ranks, -1)
    select = target[None, :] == jnp.arange(req_count * slot_cap)[:, None]
    places = jnp.sum(jnp.where(select, (dest % prompt_rows + 1)[None, :], 0), axis=1) - 1
    chooser = select.astype(jnp.bfloat16)
    outgoing = jnp.dot(chooser, merged, preferred_element_type=jnp.float32).astype(jnp.bfloat16)
    arrived, landing = (
        lax.all_to_all(
            outgoing.reshape(req_count, slot_cap, -1),
            "req",
            split_axis=0,
            concat_axis=0,
            tiled=True,
        ),
        lax.all_to_all(
            places.reshape(req_count, slot_cap), "req", split_axis=0, concat_axis=0, tiled=True
        ),
    )
    arrived = arrived.reshape(req_count * slot_cap, -1)
    landing = landing.reshape(-1)
    incoming = jnp.dot(arrived, w_merge, preferred_element_type=jnp.float32).astype(jnp.bfloat16)
    placer = landing[None, :] == jnp.arange(prompt_rows)[:, None]
    placed = jnp.dot(
        placer.astype(jnp.bfloat16), incoming, preferred_element_type=jnp.float32
    ).astype(jnp.bfloat16)
    filled = jnp.any(placer, axis=1)
    return jnp.where(filled[:, None], placed, text_embed)


def solution(mesh):
    return jax.shard_map(
        local,
        mesh=mesh,
        in_specs=(
            P("row", "req", None),
            P("row", None),
            P(),
            P(None, None, "req"),
            P("req", None),
            P(),
            P(None, "req"),
            P("req", None),
            P(),
            P(("req", "row"), None),
            P("row", "req"),
        ),
        out_specs=P(("req", "row"), None),
        check_vma=False,
    )
```

profile of v0, /device:TPU:0, one launch (start us, length us, event | category | flops | bytes accessed | tf_op | source)
XLA Modules:
  0.0 349.8 jit_solution(17088282344082328541)
XLA Ops:
  6.5 0.0 copy-start
  6.5 1.2 convert_reduce_fusion.1
  7.7 1.2 fusion.59
  8.9 1.9 fusion.61
  10.9 0.0 all-gather.3.cloned.1.call-update
  10.9 0.0 reduce-scatter.3.cloned.1.call-start
  11.0 0.6 broadcast.226
  11.5 1.4 reduce.7
  12.9 56.8 %all-gather.3.cloned.1.call-done = bf16[2048,1280]{1,0:T(8,128)(2,1)} async-done(((bf16[128,1280]{1,0:T(8,128)(2,1)}), bf16[2048,1280]{1,0:T(8,128)(2,1)}) %all-gather.3.cloned.1.call-update) | async-done | bytes 5242896 | tf_op jit(solution)/shard_map/all_gather | solution.py:41
  69.8 4.2 %fusion.105 = f32[2048,240]{0,1:S(1)} fusion(bf16[2048,1280]{1,0:T(8,128)(2,1)} %all-gather.3.cloned.1.call-done, bf16[1280,240]{0,1:T(8,128)(2,1)} %bitcast.94), kind=kOutput, calls=%fused_computation.160 | convolution fusion | flops 1258291200 | bytes 7823360
  73.9 0.1 convert_bitcast_fusion
  74.1 0.0 copy-start.4
  74.1 0.1 slice_bitcast_fusion
  74.2 0.3 copy.29
  74.4 0.3 copy.26
  74.7 0.3 copy.27
  75.0 0.0 copy-done.4
  75.0 0.0 copy-start.3
  75.0 11.0 %while.10 = (s32[]{:T(128)}, bf16[4,512,80]{1,2,0:T(8,128)(2,1)S(1)}, s32[4,512]{1,0:T(4,128)S(1)}, s32[1,2048]{1,0:T(1,128)S(1)}, bf16[4,512,80]{2,1,0:T(8,128)...) while((s32[]{:T(128)}, bf16[4,512,80]{1,2,0:T(8,128)(2,1)S(1)}, ...), condition=%wide.region_8.9_spmd, body=%wide.region_5.8_spmd.sunk | while | flops 345021440 | bytes 13869153 | solution.py:64
  75.1 0.9 fusion.125
  76.0 0.7 fusion.126
  76.7 1.1 fusion.127
  77.8 0.9 fusion.125
  78.7 0.7 fusion.126
  79.4 1.1 fusion.127
  80.6 0.9 fusion.125
  81.5 0.7 fusion.126
  82.2 1.1 fusion.127
  83.3 0.9 fusion.125
  84.2 0.7 fusion.126
  84.9 1.1 fusion.127
  86.1 3.9 %convolution_convert_fusion.1 = bf16[2048,1280]{1,0:T(8,128)(2,1)} fusion(bf16[2048,80]{0,1:T(8,128)(2,1)S(1)} %bitcast.88, bf16[80,1280]{1,0:T(8,128)(2,1)S(1)} %copy-done.3), kind=kOutput, calls=%fused_computation.13 | convolution fusion | flops 422051840 | bytes 5775360 | tf_op jit(solution)/shard_map/dot_general | solution.py:70
  90.0 0.0 reduce-scatter.3.cloned.1.call-update
  90.0 0.0 all-gather.5.cloned.1.call-start
  90.0 78.7 %reduce-scatter.3.cloned.1.call-done = bf16[128,1280]{1,0:T(8,128)(2,1)} async-done(((bf16[2048,1280]{1,0:T(8,128)(2,1)}), bf16[128,1280]{1,0:T(8,128)(2,1)}) %reduce-scatter.3.cloned.1.call-update) | async-done | bytes 327696 | tf_op jit(solution)/shard_map/reduce_scatter | solution.py:69
  168.8 0.0 copy-done.1
  168.8 1.2 convert_reduce_fusion
  170.0 0.2 fusion.56
  170.2 1.0 fusion.58
  171.2 0.0 all-gather.5.cloned.1.call-update
  171.2 0.2 reduce-scatter.5.cloned.1.call-start
  171.4 55.5 %all-gather.5.cloned.1.call-done = bf16[2048,1280]{1,0:T(8,128)(2,1)} async-done(((bf16[128,1280]{1,0:T(8,128)(2,1)}), bf16[2048,1280]{1,0:T(8,128)(2,1)}) %all-gather.5.cloned.1.call-update) | async-done | bytes 5242896 | tf_op jit(solution)/shard_map/all_gather | solution.py:79
  226.9 0.0 copy-done
  226.9 13.4 %convolution_convert_fusion = bf16[2048,1280]{1,0:T(8,128)(2,1)} fusion(bf16[320,1280]{1,0:T(8,128)(2,1)S(1)} %copy-done, bf16[2048,1280]{1,0:T(8,128)(2,1)} %all-gather.5.cloned.1.call-done, bf16[1280,320]{0,1:T(8,128)(2,1)S(1)} %copy-done.6), kind=kOutput, calls=%fused_computation.12 | convolution fusion | flops 3400663040 | bytes 12124160 | tf_op jit(solution)/shard_map/dot_general | solution.py:87
  240.3 0.0 reduce-scatter.5.cloned.1.call-update
  240.3 0.6 copy-done.7
  241.0 0.2 convert_reduce_fusion.2
  241.2 0.1 select_reduce_fusion
  241.3 0.7 sub.48
  242.0 5.3 %all-to-all-start = ((s32[16,1,2]{2,1,0:T(1,128)}), s32[16,1,2]{2,1,0:T(1,128)S(1)}, u32[]{:S(2)}, u32[]{:S(2)}) async-start(s32[16,1,2]{2,1,0:T(1,128)} %bitcast.9), calls=%async_computation | async-start | bytes 16384 | tf_op jit(solution)/shard_map/all_to_all | solution.py:115
  247.3 71.8 %reduce-scatter.5.cloned.1.call-done = bf16[128,1280]{1,0:T(8,128)(2,1)} async-done(((bf16[2048,1280]{1,0:T(8,128)(2,1)}), bf16[128,1280]{1,0:T(8,128)(2,1)}) %reduce-scatter.5.cloned.1.call-update) | async-done | bytes 327696 | tf_op jit(solution)/shard_map/reduce_scatter | solution.py:86
  319.1 1.0 fusion.63
  320.1 0.2 reshape.112
  320.3 0.2 convolution_convert_fusion.2
  320.6 0.8 reshape.113
  321.4 0.0 all-to-all-done
  321.4 4.9 %all-to-all-start.1 = ((bf16[16,2,5120]{2,1,0:T(2,128)(2,1)}), bf16[16,2,5120]{2,1,0:T(2,128)(2,1)S(1)}, u32[]{:S(2)}, u32[]{:S(2)}) async-start(bf16[16,2,5120]{2,1,0:T(2,128)(2,1)} %reshape.113), calls=%async_computation.3 | async-start | bytes 655360 | tf_op jit(solution)/shard_map/all_to_all | solution.py:108
  326.4 0.7 reduce.8
  327.1 0.1 eq.69
  327.1 0.1 fusion.64
  327.2 7.9 %all-to-all-done.1 = bf16[16,2,5120]{2,1,0:T(2,128)(2,1)S(1)} async-done(((bf16[16,2,5120]{2,1,0:T(2,128)(2,1)}), bf16[16,2,5120]{2,1,0:T(2,128)(2,1)S(1)}, u32[]{:S(2)}, u32[]{:S(2)}) %all-to-all-start.1) | async-done | bytes 327712 | tf_op jit(solution)/shard_map/all_to_all | solution.py:108
  335.2 0.1 reshape.114
  335.3 0.0 copy-done.2
  335.3 8.0 %fusion.18 = bf16[128,1280]{1,0:T(8,128)(2,1)} fusion(bf16[128,1280]{1,0:T(8,128)(2,1)S(1)} %copy-done.2, bf16[32,5120]{1,0:T(8,128)(2,1)S(1)} %reshape.114, bf16[5120,1280]{1,0:T(8,128)(2,1)} %param.21, pred[128]{0:T(512)(128)(4,1)S(1)} %fusion.64, s32[32]{0:T(128)S(1)} %eq.69), kind=kOutput, calls=%fused_computation.35 | convolution fusion | flops 430288896 | bytes 14090496 | tf_op jit(solution)/shard_map/dot_general | solution.py:123
  (24 shorter events, 0.2 us)
Async XLA Ops:
  6.5 220.4 %copy-start = (bf16[320,1280]{1,0:T(8,128)(2,1)S(1)}, bf16[320,1280]{1,0:T(8,128)(2,1)}, u32[]{:S(2)}) copy-start(bf16[320,1280]{1,0:T(8,128)(2,1)} %param.20) | copy-start | bytes 2457604
  6.5 63.2 %all-gather.3.cloned.1.call-start = ((), (), s32[]{:S(2)}) async-start(), calls=%async_computation.4 | async-start | bytes 5570560 | tf_op jit(solution)/shard_map/all_gather | solution.py:41
  10.9 157.9 %reduce-scatter.3.cloned.1.call-start = ((), (), s32[]{:S(2)}) async-start(), calls=%async_computation.5 | async-start | bytes 5570560 | tf_op jit(solution)/shard_map/reduce_scatter | solution.py:69
  74.1 0.9 copy-start.4
  75.0 11.0 %copy-start.3 = (bf16[80,1280]{1,0:T(8,128)(2,1)S(1)}, bf16[80,1280]{1,0:T(8,128)(2,1)}, u32[]{:S(2)}) copy-start(bf16[80,1280]{1,0:T(8,128)(2,1)} %param.17) | copy-start | bytes 614404
  90.0 78.8 %copy-start.1 = (bf16[1,128,1280]{2,1,0:T(8,128)(2,1)S(1)}, bf16[1,128,1280]{2,1,0:T(8,128)(2,1)}, u32[]{:S(2)}) copy-start(bf16[1,128,1280]{2,1,0:T(8,128)(2,1)} %param.13) | copy-start | bytes 983044
  90.0 80.2 %copy-start.5 = (f32[1280]{0:T(1024)S(1)}, f32[1280]{0:T(1024)}, u32[]{:S(2)}) copy-start(f32[1280]{0:T(1024)} %param.18) | copy-start | bytes 15364
  90.0 137.0 %copy-start.6 = (bf16[1280,320]{0,1:T(8,128)(2,1)S(1)}, bf16[1280,320]{0,1:T(8,128)(2,1)}, u32[]{:S(2)}) copy-start(bf16[1280,320]{0,1:T(8,128)(2,1)} %param.19) | copy-start | bytes 2457604
  90.0 136.9 %all-gather.5.cloned.1.call-start = ((), (), s32[]{:S(2)}) async-start(), calls=%async_computation.6 | async-start | bytes 5570560 | tf_op jit(solution)/shard_map/all_gather | solution.py:79
  171.2 147.9 %reduce-scatter.5.cloned.1.call-start = ((), (), s32[]{:S(2)}) async-start(), calls=%async_computation.7 | async-start | bytes 5570560 | tf_op jit(solution)/shard_map/reduce_scatter | solution.py:86
  240.3 0.7 copy-start.7
  241.0 94.3 %copy-start.2 = (bf16[128,1280]{1,0:T(8,128)(2,1)S(1)}, bf16[128,1280]{1,0:T(8,128)(2,1)}, u32[]{:S(2)}) copy-start(bf16[128,1280]{1,0:T(8,128)(2,1)} %param.22) | copy-start | bytes 983044
  242.0 79.4 %all-to-all-start = ((s32[16,1,2]{2,1,0:T(1,128)}), s32[16,1,2]{2,1,0:T(1,128)S(1)}, u32[]{:S(2)}, u32[]{:S(2)}) async-start(s32[16,1,2]{2,1,0:T(1,128)} %bitcast.9), calls=%async_computation | async-start | bytes 16384 | tf_op jit(solution)/shard_map/all_to_all | solution.py:115
  321.4 13.8 %all-to-all-start.1 = ((bf16[16,2,5120]{2,1,0:T(2,128)(2,1)}), bf16[16,2,5120]{2,1,0:T(2,128)(2,1)S(1)}, u32[]{:S(2)}, u32[]{:S(2)}) async-start(bf16[16,2,5120]{2,1,0:T(2,128)(2,1)} %reshape.113), calls=%async_computation.3 | async-start | bytes 655360 | tf_op jit(solution)/shard_map/all_to_all | solution.py:108
Sparse Core Ops, SparseCore 0:
  11.0 58.7 all-gather.2
  90.1 78.6 reduce-scatter.2
  171.3 55.5 all-gather.4
  240.5 78.5 reduce-scatter.4
where the time goes:
time: 350 us
  waiting for transfers between devices  271 us (77%)
  matrix products  37.6 us (11%)
  between operations  13.3 us (4%)
  other arithmetic  13.2 us (4%)
  starting transfers between devices  10.5 us (3%)
  local copies, waits for them, and re-layouts  4.15 us (1%)
    reduce_scatter x1, waiting for transfers between devices, local(): lax.psum_scatter(jnp.dot(piece, w_out, preferred_element_type=jnp.float32...  78.7 us
    reduce_scatter x1, waiting for transfers between devices, local(): lax.psum_scatter(jnp.dot(piece, w_down, preferred_element_type=jnp.float3...  71.8 us
    all_gather x1, waiting for transfers between devices, local(): lax.all_gather(normed, 'req', axis=0, tiled=True)  56.8 us
    all_gather x1, waiting for transfers between devices, local(): lax.all_gather(normed_two, 'req', axis=0, tiled=True)  55.5 us
    dot_general x1, matrix products, local(): jnp.dot(piece, w_down, preferred_element_type=jnp.float32)  13.4 us
    dot_general x1, matrix products, local(): jnp.dot(placer.astype(jnp.bfloat16), incoming, preferred_element_type=jnp...  7.96 us
    all_to_all x1, waiting for transfers between devices, local(): lax.all_to_all(outgoing.reshape(req_count, slot_cap, -1), 'req', split_ax...  7.94 us
  transfers between devices with their start and end apart: 6, of which 5 were waited for; matrix products, arithmetic and copies ran while one was open for 2% of the time, Pallas kernels for 0%

commit v1 on v0

--- a/solution.py
+++ b/solution.py
@@ -38,7 +38,9 @@
     normed = layer_norm(rows, ln_attn).astype(jnp.bfloat16)
     qkv = jnp.einsum(
         "rd,tdc->trc",
-        lax.all_gather(normed, "req", axis=0, tiled=True),
+        jnp.concatenate(
+            lax.all_to_all(jnp.stack([normed] * lax.axis_size("req")), "req", 0, 0), axis=0
+        ),
         w_qkv,
         preferred_element_type=jnp.float32,
     ).astype(jnp.bfloat16)

time: 350 us -> 388 us (1.11)
  waiting for transfers between devices: 271 us -> 300 us
  starting transfers between devices: 10.5 us -> 17.8 us
    all_to_all x0 -> x1, waiting for transfers between devices: none -> 77.7 us  [local(): lax.all_to_all(jnp.stack([normed] * lax.axis_size('req')), 'req', 0, 0)]
    all_gather x1 -> x0, waiting for transfers between devices: 56.8 us -> none  [local(): lax.all_gather(normed, 'req', axis=0, tiled=True)]
    reduce_scatter x1, waiting for transfers between devices: 78.7 us -> 86.6 us  [local(): lax.psum_scatter(jnp.dot(piece, w_out, preferred_element_type=jnp.float32...]
    all_to_all x0 -> x1, starting transfers between devices: none -> 7.29 us  [local(): lax.all_to_all(jnp.stack([normed] * lax.axis_size('req')), 'req', 0, 0)]
  transfers between devices with their start and end apart: 6 -> 6, of which waited for: 5 -> 5; matrix products, arithmetic and copies ran while one was open for 2% -> 1% of each run, Pallas kernels for 0% -> 0%
where the time goes in v1:
time: 388 us; the launch traced here: 387 us
  waiting for transfers between devices  300 us (77%)
  matrix products  37.4 us (10%)
  starting transfers between devices  17.8 us (5%)
  between operations  13.3 us (3%)
  other arithmetic  11.8 us (3%)
  local copies, waits for them, and re-layouts  7.01 us (2%)
    reduce_scatter x1, waiting for transfers between devices, local(): lax.psum_scatter(jnp.dot(piece, w_out, preferred_element_type=jnp.float32...  86.6 us
    all_to_all x1, waiting for transfers between devices, local(): lax.all_to_all(jnp.stack([normed] * lax.axis_size('req')), 'req', 0, 0)  77.7 us
    reduce_scatter x1, waiting for transfers between devices, local(): lax.psum_scatter(jnp.dot(piece, w_down, preferred_element_type=jnp.float3...  71.8 us
    all_gather x1, waiting for transfers between devices, local(): lax.all_gather(normed_two, 'req', axis=0, tiled=True)  55.6 us
    dot_general x1, matrix products, local(): jnp.dot(piece, w_down, preferred_element_type=jnp.float32)  13.4 us
    dot_general x1, matrix products, local(): jnp.dot(placer.astype(jnp.bfloat16), incoming, preferred_element_type=jnp...  7.95 us
    all_to_all x1, waiting for transfers between devices, local(): lax.all_to_all(outgoing.reshape(req_count, slot_cap, -1), 'req', split_ax...  7.94 us
  transfers between devices with their start and end apart: 6, of which 5 were waited for; matrix products, arithmetic and copies ran while one was open for 1% of the time, Pallas kernels for 0%

profile of v1, /device:TPU:0, one launch (start us, length us, event | category | flops | bytes accessed | tf_op | source)
XLA Modules:
  0.0 387.0 jit_solution(3475780468766617884)
XLA Ops:
  6.5 0.0 copy-start
  6.5 1.2 convert_reduce_fusion.1
  7.7 1.2 fusion.58
  8.9 1.2 fusion.64
  10.1 2.9 stack.5
  13.0 7.3 %all-to-all-start.1 = ((bf16[16,128,1280]{2,1,0:T(8,128)(2,1)}), bf16[16,128,1280]{2,1,0:T(8,128)(2,1)}, u32[]{:S(2)}, u32[]{:S(2)}) async-start(bf16[16,128,1280]{2,1,0:T(8,128)(2,1)} %stack.5), calls=%async_computation.1 | async-start | bytes 10485760 | tf_op jit(solution)/shard_map/all_to_all | solution.py:42
  20.3 0.0 reduce-scatter.3.cloned.1.call-start
  20.4 0.6 broadcast.237
  20.9 0.0 copy-done.4
  20.9 0.7 reduce.7
  21.7 77.7 %all-to-all-done.1 = bf16[16,128,1280]{2,1,0:T(8,128)(2,1)} async-done(((bf16[16,128,1280]{2,1,0:T(8,128)(2,1)}), bf16[16,128,1280]{2,1,0:T(8,128)(2,1)}, u32[]{:S(2)}, u32[]{:S(2)}) %all-to-all-start.1) | async-done | bytes 5242912 | tf_op jit(solution)/shard_map/all_to_all | solution.py:42
  99.3 4.0 %fusion.106 = f32[2048,240]{0,1:S(1)} fusion(bf16[2048,1280]{1,0:T(8,128)(2,1)} %bitcast.12, bf16[1280,240]{0,1:T(8,128)(2,1)S(1)} %bitcast.91), kind=kOutput, calls=%fused_computation.162 | convolution fusion | flops 1258291200 | bytes 7823360
  103.4 0.1 convert_bitcast_fusion
  103.5 0.1 slice_bitcast_fusion
  103.6 0.3 copy.29
  103.9 0.3 copy.26
  104.1 0.3 copy.27
  104.4 0.0 copy-start.3
  104.4 10.9 %while.10 = (s32[]{:T(128)}, bf16[4,512,80]{1,2,0:T(8,128)(2,1)S(1)}, s32[4,512]{1,0:T(4,128)S(1)}, s32[1,2048]{1,0:T(1,128)S(1)}, bf16[4,512,80]{2,1,0:T(8,128)...) while((s32[]{:T(128)}, bf16[4,512,80]{1,2,0:T(8,128)(2,1)S(1)}, ...), condition=%wide.region_8.9_spmd, body=%wide.region_5.8_spmd.sunk | while | flops 345021440 | bytes 13869153 | solution.py:66
  104.5 0.9 fusion.126
  105.4 0.7 fusion.127
  106.1 1.1 fusion.128
  107.2 0.9 fusion.126
  108.1 0.7 fusion.127
  108.8 1.1 fusion.128
  109.9 0.9 fusion.126
  110.8 0.7 fusion.127
  111.6 1.1 fusion.128
  112.7 0.9 fusion.126
  113.6 0.7 fusion.127
  114.3 1.1 fusion.128
  115.4 0.0 copy-done.3
  115.4 3.9 %convolution_convert_fusion.1 = bf16[2048,1280]{1,0:T(8,128)(2,1)} fusion(bf16[2048,80]{0,1:T(8,128)(2,1)S(1)} %bitcast.85, bf16[80,1280]{1,0:T(8,128)(2,1)S(1)} %copy-done.3), kind=kOutput, calls=%fused_computation.13 | convolution fusion | flops 422051840 | bytes 5775360 | tf_op jit(solution)/shard_map/dot_general | solution.py:72
  119.3 0.0 reduce-scatter.3.cloned.1.call-update
  119.3 0.0 all-gather.2.cloned.1.call-start
  119.4 86.6 %reduce-scatter.3.cloned.1.call-done = bf16[128,1280]{1,0:T(8,128)(2,1)} async-done(((bf16[2048,1280]{1,0:T(8,128)(2,1)}), bf16[128,1280]{1,0:T(8,128)(2,1)}) %reduce-scatter.3.cloned.1.call-update) | async-done | bytes 327696 | tf_op jit(solution)/shard_map/reduce_scatter | solution.py:71
  206.0 1.1 convert_reduce_fusion
  207.1 0.2 fusion.54
  207.4 0.0 copy-done.5
  207.4 1.0 fusion.56
  208.3 0.0 all-gather.2.cloned.1.call-update
  208.4 0.2 reduce-scatter.5.cloned.1.call-start
  208.6 55.6 %all-gather.2.cloned.1.call-done = bf16[2048,1280]{1,0:T(8,128)(2,1)} async-done(((bf16[128,1280]{1,0:T(8,128)(2,1)}), bf16[2048,1280]{1,0:T(8,128)(2,1)}) %all-gather.2.cloned.1.call-update) | async-done | bytes 5242896 | tf_op jit(solution)/shard_map/all_gather | solution.py:81
  264.1 0.0 copy-done.6
  264.2 13.4 %convolution_convert_fusion = bf16[2048,1280]{1,0:T(8,128)(2,1)} fusion(bf16[320,1280]{1,0:T(8,128)(2,1)S(1)} %copy-done, bf16[2048,1280]{1,0:T(8,128)(2,1)} %all-gather.2.cloned.1.call-done, bf16[1280,320]{0,1:T(8,128)(2,1)S(1)} %copy-done.6), kind=kOutput, calls=%fused_computation.12 | convolution fusion | flops 3400663040 | bytes 12124160 | tf_op jit(solution)/shard_map/dot_general | solution.py:89
  277.5 0.0 reduce-scatter.5.cloned.1.call-update
  277.6 0.6 copy-done.8
  278.2 0.2 convert_reduce_fusion.2
  278.4 0.1 select_reduce_fusion
  278.5 0.7 sub.53
  279.2 5.3 %all-to-all-start = ((s32[16,1,2]{2,1,0:T(1,128)}), s32[16,1,2]{2,1,0:T(1,128)S(1)}, u32[]{:S(2)}, u32[]{:S(2)}) async-start(s32[16,1,2]{2,1,0:T(1,128)} %bitcast.9), calls=%async_computation | async-start | bytes 16384 | tf_op jit(solution)/shard_map/all_to_all | solution.py:117
  284.5 71.8 %reduce-scatter.5.cloned.1.call-done = bf16[128,1280]{1,0:T(8,128)(2,1)} async-done(((bf16[2048,1280]{1,0:T(8,128)(2,1)}), bf16[128,1280]{1,0:T(8,128)(2,1)}) %reduce-scatter.5.cloned.1.call-update) | async-done | bytes 327696 | tf_op jit(solution)/shard_map/reduce_scatter | solution.py:88
  356.3 1.0 fusion.63
  357.3 0.2 reshape.137
  357.5 0.2 convolution_convert_fusion.2
  357.8 0.9 reshape.138
  358.6 0.0 all-to-all-done
  358.6 4.9 %all-to-all-start.2 = ((bf16[16,2,5120]{2,1,0:T(2,128)(2,1)}), bf16[16,2,5120]{2,1,0:T(2,128)(2,1)S(1)}, u32[]{:S(2)}, u32[]{:S(2)}) async-start(bf16[16,2,5120]{2,1,0:T(2,128)(2,1)} %reshape.138), calls=%async_computation.4 | async-start | bytes 655360 | tf_op jit(solution)/shard_map/all_to_all | solution.py:110
  363.6 0.7 reduce.8
  364.3 0.1 eq.69
  364.3 0.1 fusion.65
  364.4 7.9 %all-to-all-done.2 = bf16[16,2,5120]{2,1,0:T(2,128)(2,1)S(1)} async-done(((bf16[16,2,5120]{2,1,0:T(2,128)(2,1)}), bf16[16,2,5120]{2,1,0:T(2,128)(2,1)S(1)}, u32[]{:S(2)}, u32[]{:S(2)}) %all-to-all-start.2) | async-done | bytes 327712 | tf_op jit(solution)/shard_map/all_to_all | solution.py:110
  372.4 0.1 reshape.139
  372.5 7.9 %fusion.18 = bf16[128,1280]{1,0:T(8,128)(2,1)} fusion(bf16[128,1280]{1,0:T(8,128)(2,1)S(1)} %copy-done.2, bf16[32,5120]{1,0:T(8,128)(2,1)S(1)} %reshape.139, bf16[5120,1280]{1,0:T(8,128)(2,1)} %param.21, pred[128]{0:T(512)(128)(4,1)S(1)} %fusion.65, s32[32]{0:T(128)S(1)} %eq.69), kind=kOutput, calls=%fused_computation.35 | convolution fusion | flops 430288896 | bytes 14090496 | tf_op jit(solution)/shard_map/dot_general | solution.py:125
  (26 shorter events, 0.2 us)
Async XLA Ops:
  6.5 257.6 %copy-start = (bf16[320,1280]{1,0:T(8,128)(2,1)S(1)}, bf16[320,1280]{1,0:T(8,128)(2,1)}, u32[]{:S(2)}) copy-start(bf16[320,1280]{1,0:T(8,128)(2,1)} %param.20) | copy-start | bytes 2457604
  13.0 7.9 %copy-start.4 = (s32[1,2048]{1,0:T(1,128)S(1)}, s32[1,2048]{1,0:T(1,128)}, u32[]{:S(2)}) copy-start(s32[1,2048]{1,0:T(1,128)} %param.14) | copy-start | bytes 24580
  13.0 86.3 %copy-start.7 = (bf16[3,1280,80]{1,2,0:T(8,128)(2,1)S(1)}, bf16[3,1280,80]{1,2,0:T(8,128)(2,1)}, u32[]{:S(2)}) copy-start(bf16[3,1280,80]{1,2,0:T(8,128)(2,1)} %param.16) | copy-start | bytes 1843204
  13.0 86.3 %all-to-all-start.1 = ((bf16[16,128,1280]{2,1,0:T(8,128)(2,1)}), bf16[16,128,1280]{2,1,0:T(8,128)(2,1)}, u32[]{:S(2)}, u32[]{:S(2)}) async-start(bf16[16,128,1280]{2,1,0:T(8,128)(2,1)} %stack.5), calls=%async_computation.1 | async-start | bytes 10485760 | tf_op jit(solution)/shard_map/all_to_all | solution.py:42
  20.3 185.7 %reduce-scatter.3.cloned.1.call-start = ((), (), s32[]{:S(2)}) async-start(), calls=%async_computation.5 | async-start | bytes 5570560 | tf_op jit(solution)/shard_map/reduce_scatter | solution.py:71
  104.4 11.0 %copy-start.3 = (bf16[80,1280]{1,0:T(8,128)(2,1)S(1)}, bf16[80,1280]{1,0:T(8,128)(2,1)}, u32[]{:S(2)}) copy-start(bf16[80,1280]{1,0:T(8,128)(2,1)} %param.17) | copy-start | bytes 614404
  119.3 86.7 %copy-start.1 = (bf16[1,128,1280]{2,1,0:T(8,128)(2,1)S(1)}, bf16[1,128,1280]{2,1,0:T(8,128)(2,1)}, u32[]{:S(2)}) copy-start(bf16[1,128,1280]{2,1,0:T(8,128)(2,1)} %param.13) | copy-start | bytes 983044
  119.3 88.1 %copy-start.5 = (f32[1280]{0:T(1024)S(1)}, f32[1280]{0:T(1024)}, u32[]{:S(2)}) copy-start(f32[1280]{0:T(1024)} %param.18) | copy-start | bytes 15364
  119.3 144.8 %copy-start.6 = (bf16[1280,320]{0,1:T(8,128)(2,1)S(1)}, bf16[1280,320]{0,1:T(8,128)(2,1)}, u32[]{:S(2)}) copy-start(bf16[1280,320]{0,1:T(8,128)(2,1)} %param.19) | copy-start | bytes 2457604
  119.3 144.8 %all-gather.2.cloned.1.call-start = ((), (), s32[]{:S(2)}) async-start(), calls=%async_computation.6 | async-start | bytes 5570560 | tf_op jit(solution)/shard_map/all_gather | solution.py:81
  208.4 147.9 %reduce-scatter.5.cloned.1.call-start = ((), (), s32[]{:S(2)}) async-start(), calls=%async_computation.7 | async-start | bytes 5570560 | tf_op jit(solution)/shard_map/reduce_scatter | solution.py:88
  277.5 0.7 copy-start.8
  278.2 94.3 %copy-start.2 = (bf16[128,1280]{1,0:T(8,128)(2,1)S(1)}, bf16[128,1280]{1,0:T(8,128)(2,1)}, u32[]{:S(2)}) copy-start(bf16[128,1280]{1,0:T(8,128)(2,1)} %param.22) | copy-start | bytes 983044
  279.2 79.4 %all-to-all-start = ((s32[16,1,2]{2,1,0:T(1,128)}), s32[16,1,2]{2,1,0:T(1,128)S(1)}, u32[]{:S(2)}, u32[]{:S(2)}) async-start(s32[16,1,2]{2,1,0:T(1,128)} %bitcast.9), calls=%async_computation | async-start | bytes 16384 | tf_op jit(solution)/shard_map/all_to_all | solution.py:117
  358.6 13.8 %all-to-all-start.2 = ((bf16[16,2,5120]{2,1,0:T(2,128)(2,1)}), bf16[16,2,5120]{2,1,0:T(2,128)(2,1)S(1)}, u32[]{:S(2)}, u32[]{:S(2)}) async-start(bf16[16,2,5120]{2,1,0:T(2,128)(2,1)} %reshape.138), calls=%async_computation.4 | async-start | bytes 655360 | tf_op jit(solution)/shard_map/all_to_all | solution.py:110
Sparse Core Ops, SparseCore 0:
  119.4 86.4 reduce-scatter.2
  208.5 55.6 all-gather.1
  277.7 78.5 reduce-scatter.4
